TPU v7x, 32 devices: a whole 2x2x4 slice. The times are simulated.
32 devices in a mesh: section: 8 (over z, core), ctx: 4 (over y, x).
Axes of the slice: x: 2, y: 2, z: 4, core: 2. Of those that a mesh axis runs over, the one named last changes fastest.
Arguments:
- gate_q: bfloat16 [8, 512, 4096], P('section', 'ctx'), may hold values from -6 to 6
- gate_k: bfloat16 [8, 512, 4096], P('section', 'ctx'), may hold values from -6 to 6
- value_in: bfloat16 [8, 512, 4096], P('section', 'ctx'), may hold values from -6 to 6
- filter_raw: bfloat16 [8, 512, 4096], P('section', 'ctx'), may hold values from -0.5 to 0.5
- decay_rate: float32 [8, 4096], P('section'), may hold values from 0.25 to 16
- skip_gain: float32 [8, 4096], P('section'), may hold values from -4 to 4
- grad_out: bfloat16 [8, 512, 4096], P('section', 'ctx'), may hold values from -6 to 6
Outputs:
- grad_q: bfloat16 [8, 512, 4096], P('section', 'ctx')
- grad_k: bfloat16 [8, 512, 4096], P('section', 'ctx')
- grad_passed: bfloat16 [8, 512, 4096], P('section', 'ctx')
- filter_grad: bfloat16 [8, 512, 4096], P('section', 'ctx')
- rate_grad: float32 [8, 4096], P('section')
- skip_grad: float32 [8, 4096], P('section')
All inputs are finite; a program needn't handle non-finite values.
Results may differ from a plain program's by a relative error of at most 0.013.
Values may be sent and summed in bfloat16 or wider, within the bound.
A program may use at most 128 MiB of HBM per device.

v0:
```python
import math
import jax
import jax.numpy as jnp
from jax import lax
from jax.sharding import PartitionSpec as P

exact_mode = lax.Precision.HIGHEST


def shifted(x, axis, by):
    size = lax.axis_size(axis)
    pairs = [(i, i + by) for i in range(size) if 0 <= i + by < size]
    return lax.ppermute(x, axis, pairs)


def every_table(parts_count):
    twice = 2 * parts_count
    m_index = jnp.arange(parts_count, dtype=jnp.int32)[:, None, None]
    bin_grid = jnp.arange(twice, dtype=jnp.int32).reshape(parts_count, 2).T[None]
    angle = (m_index * bin_grid % twice).astype(jnp.float32) * (math.pi / parts_count)
    return jnp.stack([jnp.cos(angle), -jnp.sin(angle)], axis=2)


def combined_tables(slot_bins, tok_rows, fft_length):
    factor_len = fft_length // tok_rows
    row_index = jnp.arange(tok_rows, dtype=jnp.int32)
    frequency = slot_bins[:, None] + factor_len * row_index[None, :]
    product = row_index[None, :, None] * frequency[:, None, :] % fft_length
    angle = product.astype(jnp.float32) * (2.0 * math.pi / fft_length)
    cosine = jnp.cos(angle)
    sine = jnp.sin(angle)
    forward_table = jnp.stack(
        [jnp.stack([cosine, -sine], axis=2), jnp.stack([sine, cosine], axis=2)], axis=1
    )
    cos_back = jnp.transpose(cosine, (0, 2, 1))
    sin_back = jnp.transpose(sine, (0, 2, 1))
    inverse_table = jnp.stack(
        [jnp.stack([cos_back, sin_back], axis=2), jnp.stack([-sin_back, cos_back], axis=2)], axis=1
    )
    return (forward_table, inverse_table)


def spectral_middle(stack_mixed, stack_filter, stack_pulled, slot_bins, tok_rows, fft_length):
    forward_table, inverse_table = combined_tables(slot_bins, tok_rows, fft_length)

    def forward(stacked):
        return jnp.einsum(
            "spjc,spjqb->sqbc", stacked.astype(jnp.float32), forward_table, precision=exact_mode
        )

    def inverse(real_part, imag_part):
        stacked = jnp.stack([real_part, imag_part], axis=1)
        return jnp.einsum("sqbc,sqbpj->spjc", stacked, inverse_table, precision=exact_mode).astype(
            jnp.bfloat16
        )

    spec_mix = forward(stack_mixed)
    spec_fil = forward(stack_filter)
    spec_pul = forward(stack_pulled)
    mix_real, mix_imag = (spec_mix[:, 0], spec_mix[:, 1])
    fil_real, fil_imag = (spec_fil[:, 0], spec_fil[:, 1])
    pul_real, pul_imag = (spec_pul[:, 0], spec_pul[:, 1])
    folded_conv = inverse(
        fil_real * mix_real - fil_imag * mix_imag, fil_real * mix_imag + fil_imag * mix_real
    )
    folded_adj = inverse(
        fil_real * pul_real + fil_imag * pul_imag, fil_real * pul_imag - fil_imag * pul_real
    )
    folded_cor = inverse(
        mix_real * pul_real + mix_imag * pul_imag, mix_real * pul_imag - mix_imag * pul_real
    )
    return (folded_conv, folded_adj, folded_cor)


def shards(gate_q, gate_k, value_in, filter_raw, decay_rate, skip_gain, grad_out):
    parts_count = lax.axis_size("ctx")
    my_rank = lax.axis_index("ctx")
    tok_rows = gate_q.shape[1]
    channels = gate_q.shape[2]
    group_rows = tok_rows // parts_count
    seq_length = tok_rows * parts_count
    fft_length = 2 * seq_length
    positions = (my_rank * tok_rows + jnp.arange(tok_rows, dtype=jnp.int32)).astype(
        jnp.float32
    ) / seq_length
    rate_row = decay_rate[0][None, :]
    skip_row = skip_gain[0][None, :]
    envelope = jnp.exp(-rate_row * positions[:, None])
    modulated = filter_raw[0].astype(jnp.float32) * envelope
    filter_bf = modulated.astype(jnp.bfloat16)
    mixed_in = (gate_k[0].astype(jnp.float32) * value_in[0].astype(jnp.float32)).astype(
        jnp.bfloat16
    )
    pulled = (gate_q[0].astype(jnp.float32) * grad_out[0].astype(jnp.float32)).astype(jnp.bfloat16)
    block_shape = (parts_count, group_rows, channels)
    sectioned_mixed, sectioned_filter, sectioned_pulled = (
        lax.all_to_all(
            mixed_in.reshape(block_shape), "ctx", split_axis=0, concat_axis=0, tiled=True
        ),
        lax.all_to_all(
            filter_bf.reshape(block_shape), "ctx", split_axis=0, concat_axis=0, tiled=True
        ),
        lax.all_to_all(pulled.reshape(block_shape), "ctx", split_axis=0, concat_axis=0, tiled=True),
    )
    table_first = every_table(parts_count)

    def first_section(sectioned):
        return jnp.einsum(
            "mgc,mlir->lirgc", sectioned.astype(jnp.float32), table_first, precision=exact_mode
        ).astype(jnp.bfloat16)

    got_mixed, got_filter, got_pulled = (
        lax.all_to_all(
            first_section(sectioned_mixed), "ctx", split_axis=2, concat_axis=2, tiled=True
        ),
        lax.all_to_all(
            first_section(sectioned_filter), "ctx", split_axis=2, concat_axis=2, tiled=True
        ),
        lax.all_to_all(
            first_section(sectioned_pulled), "ctx", split_axis=2, concat_axis=2, tiled=True
        ),
    )

    def unpack(received):
        return received.reshape(2, 2, tok_rows, channels)

    slot_bins = 2 * my_rank + jnp.arange(2, dtype=jnp.int32)
    folded_conv, folded_adj, folded_cor = spectral_middle(
        unpack(got_mixed), unpack(got_filter), unpack(got_pulled), slot_bins, tok_rows, fft_length
    )

    def pack(folded):
        return folded.reshape(2, 2, parts_count, group_rows, channels)

    back_conv, back_adj, back_cor = (
        lax.all_to_all(pack(folded_conv), "ctx", split_axis=2, concat_axis=2, tiled=True),
        lax.all_to_all(pack(folded_adj), "ctx", split_axis=2, concat_axis=2, tiled=True),
        lax.all_to_all(pack(folded_cor), "ctx", split_axis=2, concat_axis=2, tiled=True),
    )
    table_last = table_first / fft_length

    def last_section(received):
        return jnp.einsum(
            "lirgc,mlir->mgc", received.astype(jnp.float32), table_last, precision=exact_mode
        ).astype(jnp.bfloat16)

    home_conv, home_adj, home_cor = (
        lax.all_to_all(last_section(back_conv), "ctx", split_axis=0, concat_axis=0, tiled=True),
        lax.all_to_all(last_section(back_adj), "ctx", split_axis=0, concat_axis=0, tiled=True),
        lax.all_to_all(last_section(back_cor), "ctx", split_axis=0, concat_axis=0, tiled=True),
    )
    conv_out = home_conv.reshape(tok_rows, channels).astype(jnp.float32)
    adjoint = home_adj.reshape(tok_rows, channels).astype(jnp.float32)
    filter_corr = home_cor.reshape(tok_rows, channels).astype(jnp.float32)
    mixed_f = mixed_in.astype(jnp.float32)
    pulled_f = pulled.astype(jnp.float32)
    grad_q_local = (grad_out[0].astype(jnp.float32) * (conv_out + skip_row * mixed_f)).astype(
        jnp.bfloat16
    )
    mixed_grad = adjoint + skip_row * pulled_f
    grad_k_local = (mixed_grad * value_in[0].astype(jnp.float32)).astype(jnp.bfloat16)
    passing = (mixed_grad * gate_k[0].astype(jnp.float32)).astype(jnp.bfloat16)
    passed = shifted(passing[None], "section", -1)
    filter_local = (filter_corr * envelope).astype(jnp.bfloat16)
    rate_part = -jnp.sum(positions[:, None] * filter_corr * modulated, axis=0)
    skip_part = jnp.sum(mixed_f * pulled_f, axis=0)
    rate_total, skip_total = (
        lax.psum(rate_part.astype(jnp.bfloat16), "ctx").astype(jnp.float32),
        lax.psum(skip_part.astype(jnp.bfloat16), "ctx").astype(jnp.float32),
    )
    return (
        grad_q_local[None],
        grad_k_local[None],
        passed,
        filter_local[None],
        rate_total[None],
        skip_total[None],
    )


def solution(mesh):
    in_specs = (
        P("section", "ctx", None),
        P("section", "ctx", None),
        P("section", "ctx", None),
        P("section", "ctx", None),
        P("section", None),
        P("section", None),
        P("section", "ctx", None),
    )
    out_specs = (
        P("section", "ctx", None),
        P("section", "ctx", None),
        P("section", "ctx", None),
        P("section", "ctx", None),
        P("section", None),
        P("section", None),
    )
    return jax.shard_map(shards, mesh=mesh, in_specs=in_specs, out_specs=out_specs, check_vma=False)
```

profile of v0, /device:TPU:0, one launch (start us, length us, event | category | flops | bytes accessed | tf_op | source)
XLA Modules:
  0.0 480.3 jit_solution(238260348380390639)
XLA Ops:
  13.0 10.0 %all-to-all-done = bf16[4,32,4096]{2,1,0:T(8,128)(2,1)S(1)} async-done(((bf16[4,32,4096]{2,1,0:T(8,128)(2,1)}), bf16[4,32,4096]{2,1,0:T(8,128)(2,1)S(1)}, u32[]{:S(2)}, u32[]{:S(2)}) %all-to-all-start) | async-done | bytes 1048608 | tf_op jit(solution)/shard_map/all_to_all | solution.py:100
  26.5 13.1 %all-to-all-done.6 = bf16[4,32,4096]{2,1,0:T(8,128)(2,1)S(1)} async-done(((bf16[4,32,4096]{2,1,0:T(8,128)(2,1)}), bf16[4,32,4096]{2,1,0:T(8,128)(2,1)S(1)}, u32[]{:S(2)}, u32[]{:S(2)}) %all-to-all-start.6) | async-done | bytes 1048608 | tf_op jit(solution)/shard_map/all_to_all | solution.py:103
  43.2 6.4 %convolution_convert_fusion = bf16[2,2,4,32,4096]{4,2,3,1,0:T(4,128)(2,1)S(1)} fusion(bf16[4,32,4096,1,1]{2,1,0,4,3:T(8,128)(2,1)S(1)} %bitcast.132, f32[4,2,1,4]{0,3,2,1:T(4,128)S(1)} %get-tuple-element.33, f32[4,2,1,4]{0,3,2,1:T(4,128)S(1)} %get-tuple-element.32), kind=kOutput, calls=%fused_computation.15 | convolution fusion | flops 102760512 | bytes 5243136 | tf_op jit(solution)/shard_map/mgc,mlir->lirgc/dot_general | solution.py:108
  61.2 6.4 %convolution_convert_fusion.2 = bf16[2,2,4,32,4096]{4,2,3,1,0:T(4,128)(2,1)S(1)} fusion(bf16[4,32,4096,1,1]{2,1,0,4,3:T(8,128)(2,1)S(1)} %bitcast.128, f32[4,2,1,4]{0,3,2,1:T(4,128)S(1)} %get-tuple-element.33, f32[4,2,1,4]{0,3,2,1:T(4,128)S(1)} %get-tuple-element.32), kind=kOutput, calls=%fused_computation.17 | convolution fusion | flops 102760512 | bytes 5243136 | tf_op jit(solution)/shard_map/mgc,mlir->lirgc/dot_general | solution.py:108
  71.9 36.1 %all-to-all-done.7 = bf16[2,2,4,32,4096]{4,3,1,0,2:T(8,128)(2,1)} async-done(((bf16[2,2,4,32,4096]{4,3,1,0,2:T(8,128)(2,1)}), bf16[2,2,4,32,4096]{4,3,1,0,2:T(8,128)(2,1)}, u32[]{:S(2)}, u32[]{:S(2)}) %all-to-all-start.7) | async-done | bytes 4194336 | tf_op jit(solution)/shard_map/all_to_all | solution.py:119
  113.1 6.4 %convolution_convert_fusion.1 = bf16[2,2,4,32,4096]{4,2,3,1,0:T(4,128)(2,1)S(1)} fusion(bf16[4,32,4096,1,1]{2,1,0,4,3:T(8,128)(2,1)S(1)} %bitcast.130, f32[4,2,1,4]{0,3,2,1:T(4,128)S(1)} %get-tuple-element.33, f32[4,2,1,4]{0,3,2,1:T(4,128)S(1)} %get-tuple-element.32), kind=kOutput, calls=%fused_computation.16 | convolution fusion | flops 102760512 | bytes 5243136 | tf_op jit(solution)/shard_map/mgc,mlir->lirgc/dot_general | solution.py:108
  123.8 36.2 %all-to-all-done.1 = bf16[2,2,4,32,4096]{4,3,1,0,2:T(8,128)(2,1)} async-done(((bf16[2,2,4,32,4096]{4,3,1,0,2:T(8,128)(2,1)}), bf16[2,2,4,32,4096]{4,3,1,0,2:T(8,128)(2,1)}, u32[]{:S(2)}, u32[]{:S(2)}) %all-to-all-start.1) | async-done | bytes 4194336 | tf_op jit(solution)/shard_map/all_to_all | solution.py:116
  182.8 29.4 %all-to-all-done.3 = bf16[2,2,4,32,4096]{4,3,1,0,2:T(8,128)(2,1)} async-done(((bf16[2,2,4,32,4096]{4,3,1,0,2:T(8,128)(2,1)}), bf16[2,2,4,32,4096]{4,3,1,0,2:T(8,128)(2,1)}, u32[]{:S(2)}, u32[]{:S(2)}) %all-to-all-start.3) | async-done | bytes 4194336 | tf_op jit(solution)/shard_map/all_to_all | solution.py:113
  220.5 11.1 %multiply_add_fusion = (f32[2,1,128,4096]{3,2,1,0:T(8,128)S(1)}, f32[2,1,128,4096]{3,2,1,0:T(8,128)}, f32[2,1,128,4096]{3,2,1,0:T(8,128)}, f32[2,1,128,4096]{3,2,1,0:T(8,128)}) fusion(f32[2,2,128,4096]{3,2,1,0:T(8,128)} %convolution_bitcast_fusion, f32[2,2,128,4096]{3,2,1,0:T(8,128)} %convolution_bitcast_fusion.1, f32[2,2,128,4096]{3,2,1,0:T(8,128)S(1)} %bitcast.118), kind=kLoop, calls=%fused_computation.25 | loop fusion | flops 12582912 | bytes 41943040 | tf_op jit(solution)/shard_map/add | solution.py:70
  231.7 7.5 %maximum_bitcast_fusion = (f32[2,2,128,4096,1]{3,2,1,0,4:T(8,128)S(1)}, f32[2,2,128,4096,1]{3,2,1,0,4:T(8,128)}) fusion(f32[2,1,128,4096]{3,2,1,0:T(8,128)} %get-tuple-element.17, f32[2,1,128,4096]{3,2,1,0:T(8,128)} %get-tuple-element.18, f32[2,1,128,4096]{3,2,1,0:T(8,128)} %get-tuple-element.12, f32[2,1,128,4096]{3,2,1,0:T(8,128)S(1)} %get-tuple-element.11), kind=kLoop, calls=%fused_computation | loop fusion | flops 4194304 | bytes 33554432 | tf_op jit(solution)/shard_map/stack | solution.py:52
  239.2 8.0 %fusion.4 = bf16[2,2,128,4096,1]{3,2,1,0,4:T(8,128)(2,1)S(1)} fusion(f32[2,2,128,4096,1]{3,2,1,0,4:T(8,128)S(1)} %get-tuple-element.34, f32[2,1,128,2,128]{2,4,3,0,1:T(8,128)S(1)} %get-tuple-element.22, f32[2,1,128,2,128]{2,4,3,0,1:T(8,128)S(1)} %get-tuple-element.21), kind=kOutput, calls=%fused_computation.10 | convolution fusion | flops 6442582016 | bytes 13107200 | tf_op jit(solution)/shard_map/sqbc,sqbpj->spjc/dot_general | solution.py:53
  247.6 6.3 %copy.51 = bf16[2,2,4,32,4096]{4,0,1,3,2:T(2,128)(2,1)} copy(bf16[2,2,4,32,4096]{4,3,2,0,1:T(8,128)(2,1)S(1)} %bitcast.122) | data formatting | bytes 8388608 | tf_op jit(solution)/shard_map/reshape | solution.py:133
  259.1 9.2 %fusion = bf16[2,2,128,4096,1]{3,2,1,0,4:T(8,128)(2,1)S(1)} fusion(f32[2,2,128,4096,1]{3,2,1,0,4:T(8,128)} %get-tuple-element.35, f32[2,1,128,2,128]{2,4,3,0,1:T(8,128)S(1)} %get-tuple-element.22, f32[2,1,128,2,128]{2,4,3,0,1:T(8,128)S(1)} %get-tuple-element.21), kind=kOutput, calls=%fused_computation.4 | convolution fusion | flops 6442582016 | bytes 13107200 | tf_op jit(solution)/shard_map/sqbc,sqbpj->spjc/dot_general | solution.py:53
  268.8 6.4 %copy.66 = bf16[2,2,4,32,4096]{4,0,1,3,2:T(2,128)(2,1)} copy(bf16[2,2,4,32,4096]{4,3,2,0,1:T(8,128)(2,1)S(1)} %bitcast.123) | data formatting | bytes 8388608 | tf_op jit(solution)/shard_map/reshape | solution.py:133
  275.2 30.8 %all-to-all-done.4 = bf16[2,2,4,32,4096]{4,0,1,3,2:T(2,128)(2,1)} async-done(((bf16[2,2,4,32,4096]{4,0,1,3,2:T(2,128)(2,1)}), bf16[2,2,4,32,4096]{4,0,1,3,2:T(2,128)(2,1)}, u32[]{:S(2)}, u32[]{:S(2)}) %all-to-all-start.4) | async-done | bytes 4194336 | tf_op jit(solution)/shard_map/all_to_all | solution.py:136
  311.1 6.5 %multiply_add_fusion.1 = (f32[2,1,128,4096]{3,2,1,0:T(8,128)S(1)}, f32[2,1,128,4096]{3,2,1,0:T(8,128)S(1)}) fusion(f32[2,2,128,4096]{3,2,1,0:T(8,128)} %convolution_bitcast_fusion, f32[2,2,128,4096]{3,2,1,0:T(8,128)} %convolution_bitcast_fusion.2), kind=kLoop, calls=%fused_computation.27 | loop fusion | flops 6291456 | bytes 25165824 | tf_op jit(solution)/shard_map/add | solution.py:67
  317.7 7.8 %fusion.2 = bf16[2,2,128,4096,1]{3,2,1,0,4:T(8,128)(2,1)S(1)} fusion(f32[2,1,128,2,128]{2,4,3,0,1:T(8,128)S(1)} %get-tuple-element.22, f32[2,1,128,2,128]{2,4,3,0,1:T(8,128)S(1)} %get-tuple-element.21, f32[2,1,128,4096]{3,2,1,0:T(8,128)S(1)} %get-tuple-element.14, f32[2,1,128,4096]{3,2,1,0:T(8,128)S(1)} %get-tuple-element.13), kind=kOutput, calls=%fused_computation.7 | convolution fusion | flops 6444679168 | bytes 13107200 | tf_op jit(solution)/shard_map/sqbc,sqbpj->spjc/dot_general | solution.py:53
  326.0 6.3 %copy.60 = bf16[2,2,4,32,4096]{4,0,1,3,2:T(2,128)(2,1)} copy(bf16[2,2,4,32,4096]{4,3,2,0,1:T(8,128)(2,1)S(1)} %bitcast.124) | data formatting | bytes 8388608 | tf_op jit(solution)/shard_map/reshape | solution.py:133
  332.3 25.7 %all-to-all-done.10 = bf16[2,2,4,32,4096]{4,0,1,3,2:T(2,128)(2,1)} async-done(((bf16[2,2,4,32,4096]{4,0,1,3,2:T(2,128)(2,1)}), bf16[2,2,4,32,4096]{4,0,1,3,2:T(2,128)(2,1)}, u32[]{:S(2)}, u32[]{:S(2)}) %all-to-all-start.10) | async-done | bytes 4194336 | tf_op jit(solution)/shard_map/all_to_all | solution.py:138
  363.4 10.8 %fusion.6 = bf16[4,32,4096]{2,0,1:T(4,128)(2,1)S(1)} fusion(bf16[2,2,4,32,4096]{4,0,1,3,2:T(2,128)(2,1)} %all-to-all-done.4, f32[4,2,1,4]{0,3,2,1:T(4,128)S(1)} %get-tuple-element.33, f32[4,2,1,4]{0,3,2,1:T(4,128)S(1)} %get-tuple-element.32), kind=kOutput, calls=%fused_computation.21 | convolution fusion | flops 101187712 | bytes 5243136 | tf_op jit(solution)/shard_map/lirgc,mlir->mgc/dot_general | solution.py:143
  375.7 34.5 %all-to-all-done.8 = bf16[2,2,4,32,4096]{4,0,1,3,2:T(2,128)(2,1)} async-done(((bf16[2,2,4,32,4096]{4,0,1,3,2:T(2,128)(2,1)}), bf16[2,2,4,32,4096]{4,0,1,3,2:T(2,128)(2,1)}, u32[]{:S(2)}, u32[]{:S(2)}) %all-to-all-start.8) | async-done | bytes 4194336 | tf_op jit(solution)/shard_map/all_to_all | solution.py:137
  413.8 10.8 %fusion.7 = bf16[4,32,4096]{2,0,1:T(4,128)(2,1)S(1)} fusion(bf16[2,2,4,32,4096]{4,0,1,3,2:T(2,128)(2,1)} %all-to-all-done.8, f32[4,2,1,4]{0,3,2,1:T(4,128)S(1)} %get-tuple-element.33, f32[4,2,1,4]{0,3,2,1:T(4,128)S(1)} %get-tuple-element.32), kind=kOutput, calls=%fused_computation.22 | convolution fusion | flops 101187712 | bytes 5243136 | tf_op jit(solution)/shard_map/lirgc,mlir->mgc/dot_general | solution.py:143
  430.6 10.8 %fusion.8 = bf16[4,32,4096]{2,0,1:T(4,128)(2,1)S(1)} fusion(bf16[2,2,4,32,4096]{4,0,1,3,2:T(2,128)(2,1)} %all-to-all-done.10, f32[4,2,1,4]{0,3,2,1:T(4,128)S(1)} %get-tuple-element.33, f32[4,2,1,4]{0,3,2,1:T(4,128)S(1)} %get-tuple-element.32), kind=kOutput, calls=%fused_computation.23 | convolution fusion | flops 101187712 | bytes 5243136 | tf_op jit(solution)/shard_map/lirgc,mlir->mgc/dot_general | solution.py:143
  461.0 15.3 %all-reduce = (bf16[1,4096]{1,0:T(2,128)(2,1)S(1)}, bf16[1,4096]{1,0:T(2,128)(2,1)S(1)}) all-reduce(bf16[1,4096]{1,0:T(2,128)(2,1)S(1)} %broadcast_in_dim.10, bf16[1,4096]{1,0:T(2,128)(2,1)S(1)} %broadcast_in_dim.12), channel_id=1, replica_groups=mesh['section'=8,'ctx'=4] {'ctx'}, use_global_device_ids=true, to_apply=%region_1.2 | all-reduce | flops 8192 | bytes 32768 | tf_op jit(solution)/shard_map/psum | solution.py:168
  (71 shorter events, 127.1 us)
Async XLA Ops:
  0.6 8.7 %copy-start.3 = (bf16[1,128,4096]{2,1,0:T(8,128)(2,1)S(1)}, bf16[1,128,4096]{2,1,0:T(8,128)(2,1)}, u32[]{:S(2)}) copy-start(bf16[1,128,4096]{2,1,0:T(8,128)(2,1)} %param.13) | copy-start | bytes 3145732
  0.6 8.7 %copy-start.2 = (bf16[1,128,4096]{2,1,0:T(8,128)(2,1)S(1)}, bf16[1,128,4096]{2,1,0:T(8,128)(2,1)}, u32[]{:S(2)}) copy-start(bf16[1,128,4096]{2,1,0:T(8,128)(2,1)} %param.8) | copy-start | bytes 3145732
  4.2 18.8 %all-to-all-start = ((bf16[4,32,4096]{2,1,0:T(8,128)(2,1)}), bf16[4,32,4096]{2,1,0:T(8,128)(2,1)S(1)}, u32[]{:S(2)}, u32[]{:S(2)}) async-start(bf16[4,32,4096]{2,1,0:T(8,128)(2,1)} %fusion.21), calls=%async_computation | async-start | bytes 2097152 | tf_op jit(solution)/shard_map/all_to_all | solution.py:100
  23.0 16.6 %all-to-all-start.6 = ((bf16[4,32,4096]{2,1,0:T(8,128)(2,1)}), bf16[4,32,4096]{2,1,0:T(8,128)(2,1)S(1)}, u32[]{:S(2)}, u32[]{:S(2)}) async-start(bf16[4,32,4096]{2,1,0:T(8,128)(2,1)} %bitcast.32), calls=%async_computation.6 | async-start | bytes 2097152 | tf_op jit(solution)/shard_map/all_to_all | solution.py:103
  39.6 16.6 %all-to-all-start.2 = ((bf16[4,32,4096]{2,1,0:T(8,128)(2,1)}), bf16[4,32,4096]{2,1,0:T(8,128)(2,1)S(1)}, u32[]{:S(2)}, u32[]{:S(2)}) async-start(bf16[4,32,4096]{2,1,0:T(8,128)(2,1)} %bitcast.17), calls=%async_computation.2 | async-start | bytes 2097152 | tf_op jit(solution)/shard_map/all_to_all | solution.py:97
  56.2 51.9 %all-to-all-start.7 = ((bf16[2,2,4,32,4096]{4,3,1,0,2:T(8,128)(2,1)}), bf16[2,2,4,32,4096]{4,3,1,0,2:T(8,128)(2,1)}, u32[]{:S(2)}, u32[]{:S(2)}) async-start(bf16[2,2,4,32,4096]{4,3,1,0,2:T(8,128)(2,1)} %copy.56), calls=%async_computation.7 | async-start | bytes 8388608 | tf_op jit(solution)/shard_map/all_to_all | solution.py:119
  108.0 52.0 %all-to-all-start.1 = ((bf16[2,2,4,32,4096]{4,3,1,0,2:T(8,128)(2,1)}), bf16[2,2,4,32,4096]{4,3,1,0,2:T(8,128)(2,1)}, u32[]{:S(2)}, u32[]{:S(2)}) async-start(bf16[2,2,4,32,4096]{4,3,1,0,2:T(8,128)(2,1)} %copy.44), calls=%async_computation.1 | async-start | bytes 8388608 | tf_op jit(solution)/shard_map/all_to_all | solution.py:116
  160.0 52.2 %all-to-all-start.3 = ((bf16[2,2,4,32,4096]{4,3,1,0,2:T(8,128)(2,1)}), bf16[2,2,4,32,4096]{4,3,1,0,2:T(8,128)(2,1)}, u32[]{:S(2)}, u32[]{:S(2)}) async-start(bf16[2,2,4,32,4096]{4,3,1,0,2:T(8,128)(2,1)} %copy.47), calls=%async_computation.3 | async-start | bytes 8388608 | tf_op jit(solution)/shard_map/all_to_all | solution.py:113
  212.2 8.3 %slice-start = ((s8[8388608]{0:T(1024)(128)(4,1)}), s8[4194304]{0:T(1024)(128)(4,1)S(1)}, s32[]{:S(2)}) async-start(s8[8388608]{0:T(1024)(128)(4,1)} %bitcast.117), calls=%async_computation.12 | async-start | bytes 8388608
  214.8 5.7 %slice-start.1 = ((s8[8388608]{0:T(1024)(128)(4,1)}), s8[4194304]{0:T(1024)(128)(4,1)S(1)}, s32[]{:S(2)}) async-start(s8[8388608]{0:T(1024)(128)(4,1)} %bitcast.117), calls=%async_computation.13 | async-start | bytes 8388608
  254.0 52.0 %all-to-all-start.4 = ((bf16[2,2,4,32,4096]{4,0,1,3,2:T(2,128)(2,1)}), bf16[2,2,4,32,4096]{4,0,1,3,2:T(2,128)(2,1)}, u32[]{:S(2)}, u32[]{:S(2)}) async-start(bf16[2,2,4,32,4096]{4,0,1,3,2:T(2,128)(2,1)} %copy.51), calls=%async_computation.4 | async-start | bytes 8388608 | tf_op jit(solution)/shard_map/all_to_all | solution.py:136
  306.0 52.0 %all-to-all-start.10 = ((bf16[2,2,4,32,4096]{4,0,1,3,2:T(2,128)(2,1)}), bf16[2,2,4,32,4096]{4,0,1,3,2:T(2,128)(2,1)}, u32[]{:S(2)}, u32[]{:S(2)}) async-start(bf16[2,2,4,32,4096]{4,0,1,3,2:T(2,128)(2,1)} %copy.66), calls=%async_computation.10 | async-start | bytes 8388608 | tf_op jit(solution)/shard_map/all_to_all | solution.py:138
  358.0 52.3 %all-to-all-start.8 = ((bf16[2,2,4,32,4096]{4,0,1,3,2:T(2,128)(2,1)}), bf16[2,2,4,32,4096]{4,0,1,3,2:T(2,128)(2,1)}, u32[]{:S(2)}, u32[]{:S(2)}) async-start(bf16[2,2,4,32,4096]{4,0,1,3,2:T(2,128)(2,1)} %copy.60), calls=%async_computation.8 | async-start | bytes 8388608 | tf_op jit(solution)/shard_map/all_to_all | solution.py:137
  410.2 16.6 %all-to-all-start.5 = ((bf16[4,32,4096]{2,1,0:T(8,128)(2,1)}), bf16[4,32,4096]{2,1,0:T(8,128)(2,1)S(1)}, u32[]{:S(2)}, u32[]{:S(2)}) async-start(bf16[4,32,4096]{2,1,0:T(8,128)(2,1)} %copy.54), calls=%async_computation.5 | async-start | bytes 2097152 | tf_op jit(solution)/shard_map/all_to_all | solution.py:148
  426.9 16.7 %all-to-all-start.9 = ((bf16[4,32,4096]{2,1,0:T(8,128)(2,1)}), bf16[4,32,4096]{2,1,0:T(8,128)(2,1)S(1)}, u32[]{:S(2)}, u32[]{:S(2)}) async-start(bf16[4,32,4096]{2,1,0:T(8,128)(2,1)} %copy.63), calls=%async_computation.9 | async-start | bytes 2097152 | tf_op jit(solution)/shard_map/all_to_all | solution.py:149
  441.4 5.7 %copy-start.4 = (f32[1,4096]{1,0:T(1,128)S(1)}, f32[1,4096]{1,0:T(1,128)}, u32[]{:S(2)}) copy-start(f32[1,4096]{1,0:T(1,128)} %param.12) | copy-start | bytes 49156
  443.6 3.6 copy-start.1
  443.6 16.6 %all-to-all-start.11 = ((bf16[4,32,4096]{2,1,0:T(8,128)(2,1)}), bf16[4,32,4096]{2,1,0:T(8,128)(2,1)S(1)}, u32[]{:S(2)}, u32[]{:S(2)}) async-start(bf16[4,32,4096]{2,1,0:T(8,128)(2,1)} %copy.69), calls=%async_computation.11 | async-start | bytes 2097152 | tf_op jit(solution)/shard_map/all_to_all | solution.py:150
  447.2 13.0 %copy-start = (bf16[1,128,4096]{2,1,0:T(8,128)(2,1)S(1)}, bf16[1,128,4096]{2,1,0:T(8,128)(2,1)}, u32[]{:S(2)}) copy-start(bf16[1,128,4096]{2,1,0:T(8,128)(2,1)} %param.10) | copy-start | bytes 3145732
  452.7 26.4 %collective-permute-start = (bf16[1,128,4096]{2,1,0:T(8,128)(2,1)}, bf16[1,128,4096]{2,1,0:T(8,128)(2,1)S(1)}, u32[]{:S(2)}, u32[]{:S(2)}) collective-permute-start(bf16[1,128,4096]{2,1,0:T(8,128)(2,1)} %get-tuple-element.19), channel_id=1, source_target_pairs={{4,0},{8,4},{12,8},{16,12},{20,16},{24,20},{28,24},{5,1},{9,5},{13... | collective-permute-start | bytes 3145736 | tf_op jit(solution)/shard_map/ppermute | solution.py:13
where the time goes:
time: 489 us; the launch traced here: 480 us
  waiting for transfers between devices  226 us (46%)
  matrix products  93.4 us (19%)
  starting transfers between devices  55.3 us (11%)
  local copies, waits for them, and re-layouts  46.6 us (10%)
  other arithmetic  42.8 us (9%)
  blocking collectives  15.3 us (3%)
    all_to_all x1, waiting for transfers between devices, shards(): lax.all_to_all(first_section(sectioned_filter), 'ctx', split_axis=2, conc...  36.2 us
    all_to_all x1, waiting for transfers between devices, shards(): lax.all_to_all(first_section(sectioned_pulled), 'ctx', split_axis=2, conc...  36.1 us
    all_to_all x1, waiting for transfers between devices, shards(): lax.all_to_all(pack(folded_adj), 'ctx', split_axis=2, concat_axis=2, tile...  34.5 us
    dot_general x3, matrix products, last_section(): jnp.einsum('lirgc,mlir->mgc', received.astype(jnp.float32), table_last, p...  32.4 us
    all_to_all x1, waiting for transfers between devices, shards(): lax.all_to_all(pack(folded_conv), 'ctx', split_axis=2, concat_axis=2, til...  30.8 us
    all_to_all x1, waiting for transfers between devices, shards(): lax.all_to_all(first_section(sectioned_mixed), 'ctx', split_axis=2, conca...  29.4 us
    all_to_all x1, waiting for transfers between devices, shards(): lax.all_to_all(pack(folded_cor), 'ctx', split_axis=2, concat_axis=2, tile...  25.7 us
    dot_general x3, matrix products, inverse(): jnp.einsum('sqbc,sqbpj->spjc', stacked, inverse_table, precision=exact_mode)  25 us
  transfers between devices with their start and end apart: 13, of which 12 were waited for; matrix products, arithmetic and copies ran while one was open for 28% of the time, Pallas kernels for 0%

commit v1 on v0

--- a/solution.py
+++ b/solution.py
@@ -165,7 +165,7 @@
     rate_part = -jnp.sum(positions[:, None] * filter_corr * modulated, axis=0)
     skip_part = jnp.sum(mixed_f * pulled_f, axis=0)
     rate_total, skip_total = (
-        lax.psum(rate_part.astype(jnp.bfloat16), "ctx").astype(jnp.float32),
+        jnp.sum(lax.all_gather(rate_part.astype(jnp.bfloat16), "ctx"), axis=0).astype(jnp.float32),
         lax.psum(skip_part.astype(jnp.bfloat16), "ctx").astype(jnp.float32),
     )
     return (

time: 489 us -> 500 us (1.022)
  blocking collectives: 15.3 us -> 30.5 us
    all_gather x0 -> x1, blocking collectives: none -> 8.16 us  [shards(): lax.all_gather(rate_part.astype(jnp.bfloat16), 'ctx')]
    psum x1, blocking collectives: 15.3 us -> 22.3 us  [shards(): lax.psum(skip_part.astype(jnp.bfloat16), 'ctx').astype(jnp.float32)]
  transfers between devices with their start and end apart: 13 -> 13, of which waited for: 12 -> 11; matrix products, arithmetic and copies ran while one was open for 28% -> 28% of each run, Pallas kernels for 0% -> 0%
where the time goes in v1:
time: 500 us; the launch traced here: 491 us
  waiting for transfers between devices  222 us (44%)
  matrix products  93.5 us (19%)
  starting transfers between devices  55 us (11%)
  local copies, waits for them, and re-layouts  46.6 us (9%)
  other arithmetic  42.9 us (9%)
  blocking collectives  30.5 us (6%)
    all_to_all x1, waiting for transfers between devices, shards(): lax.all_to_all(first_section(sectioned_filter), 'ctx', split_axis=2, conc...  36.2 us
    all_to_all x1, waiting for transfers between devices, shards(): lax.all_to_all(first_section(sectioned_pulled), 'ctx', split_axis=2, conc...  36.2 us
    all_to_all x1, waiting for transfers between devices, shards(): lax.all_to_all(pack(folded_adj), 'ctx', split_axis=2, concat_axis=2, tile...  34.5 us
    dot_general x3, matrix products, last_section(): jnp.einsum('lirgc,mlir->mgc', received.astype(jnp.float32), table_last, p...  32.4 us
    all_to_all x1, waiting for transfers between devices, shards(): lax.all_to_all(pack(folded_conv), 'ctx', split_axis=2, concat_axis=2, til...  30.8 us
    all_to_all x1, waiting for transfers between devices, shards(): lax.all_to_all(first_section(sectioned_mixed), 'ctx', split_axis=2, conca...  29.4 us
    all_to_all x1, waiting for transfers between devices, shards(): lax.all_to_all(pack(folded_cor), 'ctx', split_axis=2, concat_axis=2, tile...  25.7 us
    dot_general x3, matrix products, inverse(): jnp.einsum('sqbc,sqbpj->spjc', stacked, inverse_table, precision=exact_mode)  25 us
  transfers between devices with their start and end apart: 13, of which 11 were waited for; matrix products, arithmetic and copies ran while one was open for 28% of the time, Pallas kernels for 0%

profile of v1, /device:TPU:0, one launch (start us, length us, event | category | flops | bytes accessed | tf_op | source)
XLA Modules:
  0.0 491.3 jit_solution(758037344752742616)
XLA Ops:
  13.0 10.0 %all-to-all-done = bf16[4,32,4096]{2,1,0:T(8,128)(2,1)S(1)} async-done(((bf16[4,32,4096]{2,1,0:T(8,128)(2,1)}), bf16[4,32,4096]{2,1,0:T(8,128)(2,1)S(1)}, u32[]{:S(2)}, u32[]{:S(2)}) %all-to-all-start) | async-done | bytes 1048608 | tf_op jit(solution)/shard_map/all_to_all | solution.py:100
  26.5 13.1 %all-to-all-done.6 = bf16[4,32,4096]{2,1,0:T(8,128)(2,1)S(1)} async-done(((bf16[4,32,4096]{2,1,0:T(8,128)(2,1)}), bf16[4,32,4096]{2,1,0:T(8,128)(2,1)S(1)}, u32[]{:S(2)}, u32[]{:S(2)}) %all-to-all-start.6) | async-done | bytes 1048608 | tf_op jit(solution)/shard_map/all_to_all | solution.py:103
  43.2 6.4 %convolution_convert_fusion = bf16[2,2,4,32,4096]{4,2,3,1,0:T(4,128)(2,1)S(1)} fusion(bf16[4,32,4096,1,1]{2,1,0,4,3:T(8,128)(2,1)S(1)} %bitcast.133, f32[4,2,1,4]{0,3,2,1:T(4,128)S(1)} %get-tuple-element.31, f32[4,2,1,4]{0,3,2,1:T(4,128)S(1)} %get-tuple-element.30), kind=kOutput, calls=%fused_computation.15 | convolution fusion | flops 102760512 | bytes 5243136 | tf_op jit(solution)/shard_map/mgc,mlir->lirgc/dot_general | solution.py:108
  61.2 6.4 %convolution_convert_fusion.2 = bf16[2,2,4,32,4096]{4,2,3,1,0:T(4,128)(2,1)S(1)} fusion(bf16[4,32,4096,1,1]{2,1,0,4,3:T(8,128)(2,1)S(1)} %bitcast.130, f32[4,2,1,4]{0,3,2,1:T(4,128)S(1)} %get-tuple-element.31, f32[4,2,1,4]{0,3,2,1:T(4,128)S(1)} %get-tuple-element.30), kind=kOutput, calls=%fused_computation.17 | convolution fusion | flops 102760512 | bytes 5243136 | tf_op jit(solution)/shard_map/mgc,mlir->lirgc/dot_general | solution.py:108
  71.9 36.2 %all-to-all-done.7 = bf16[2,2,4,32,4096]{4,3,1,0,2:T(8,128)(2,1)} async-done(((bf16[2,2,4,32,4096]{4,3,1,0,2:T(8,128)(2,1)}), bf16[2,2,4,32,4096]{4,3,1,0,2:T(8,128)(2,1)}, u32[]{:S(2)}, u32[]{:S(2)}) %all-to-all-start.7) | async-done | bytes 4194336 | tf_op jit(solution)/shard_map/all_to_all | solution.py:119
  113.1 6.4 %convolution_convert_fusion.1 = bf16[2,2,4,32,4096]{4,2,3,1,0:T(4,128)(2,1)S(1)} fusion(bf16[4,32,4096,1,1]{2,1,0,4,3:T(8,128)(2,1)S(1)} %bitcast.131, f32[4,2,1,4]{0,3,2,1:T(4,128)S(1)} %get-tuple-element.31, f32[4,2,1,4]{0,3,2,1:T(4,128)S(1)} %get-tuple-element.30), kind=kOutput, calls=%fused_computation.16 | convolution fusion | flops 102760512 | bytes 5243136 | tf_op jit(solution)/shard_map/mgc,mlir->lirgc/dot_general | solution.py:108
  123.8 36.2 %all-to-all-done.1 = bf16[2,2,4,32,4096]{4,3,1,0,2:T(8,128)(2,1)} async-done(((bf16[2,2,4,32,4096]{4,3,1,0,2:T(8,128)(2,1)}), bf16[2,2,4,32,4096]{4,3,1,0,2:T(8,128)(2,1)}, u32[]{:S(2)}, u32[]{:S(2)}) %all-to-all-start.1) | async-done | bytes 4194336 | tf_op jit(solution)/shard_map/all_to_all | solution.py:116
  182.8 29.4 %all-to-all-done.3 = bf16[2,2,4,32,4096]{4,3,1,0,2:T(8,128)(2,1)} async-done(((bf16[2,2,4,32,4096]{4,3,1,0,2:T(8,128)(2,1)}), bf16[2,2,4,32,4096]{4,3,1,0,2:T(8,128)(2,1)}, u32[]{:S(2)}, u32[]{:S(2)}) %all-to-all-start.3) | async-done | bytes 4194336 | tf_op jit(solution)/shard_map/all_to_all | solution.py:113
  220.5 11.2 %multiply_add_fusion = (f32[2,1,128,4096]{3,2,1,0:T(8,128)S(1)}, f32[2,1,128,4096]{3,2,1,0:T(8,128)}, f32[2,1,128,4096]{3,2,1,0:T(8,128)}, f32[2,1,128,4096]{3,2,1,0:T(8,128)}) fusion(f32[2,2,128,4096]{3,2,1,0:T(8,128)} %convolution_bitcast_fusion, f32[2,2,128,4096]{3,2,1,0:T(8,128)} %convolution_bitcast_fusion.1, f32[2,2,128,4096]{3,2,1,0:T(8,128)S(1)} %bitcast.119), kind=kLoop, calls=%fused_computation.25 | loop fusion | flops 12582912 | bytes 41943040 | tf_op jit(solution)/shard_map/add | solution.py:70
  231.7 7.5 %maximum_bitcast_fusion = (f32[2,2,128,4096,1]{3,2,1,0,4:T(8,128)S(1)}, f32[2,2,128,4096,1]{3,2,1,0,4:T(8,128)}) fusion(f32[2,1,128,4096]{3,2,1,0:T(8,128)} %get-tuple-element.15, f32[2,1,128,4096]{3,2,1,0:T(8,128)} %get-tuple-element.16, f32[2,1,128,4096]{3,2,1,0:T(8,128)} %get-tuple-element.10, f32[2,1,128,4096]{3,2,1,0:T(8,128)S(1)} %get-tuple-element.9), kind=kLoop, calls=%fused_computation | loop fusion | flops 4194304 | bytes 33554432 | tf_op jit(solution)/shard_map/stack | solution.py:52
  239.2 8.0 %fusion.4 = bf16[2,2,128,4096,1]{3,2,0,1,4:T(8,128)(2,1)S(1)} fusion(f32[2,2,128,4096,1]{3,2,1,0,4:T(8,128)S(1)} %get-tuple-element.32, f32[2,1,128,2,128]{2,4,3,0,1:T(8,128)S(1)} %get-tuple-element.20, f32[2,1,128,2,128]{2,4,3,0,1:T(8,128)S(1)} %get-tuple-element.19), kind=kOutput, calls=%fused_computation.10 | convolution fusion | flops 6442582016 | bytes 13107200 | tf_op jit(solution)/shard_map/sqbc,sqbpj->spjc/dot_general | solution.py:53
  259.1 9.2 %fusion = bf16[2,2,128,4096,1]{3,2,0,1,4:T(8,128)(2,1)S(1)} fusion(f32[2,2,128,4096,1]{3,2,1,0,4:T(8,128)} %get-tuple-element.33, f32[2,1,128,2,128]{2,4,3,0,1:T(8,128)S(1)} %get-tuple-element.20, f32[2,1,128,2,128]{2,4,3,0,1:T(8,128)S(1)} %get-tuple-element.19), kind=kOutput, calls=%fused_computation.4 | convolution fusion | flops 6442582016 | bytes 13107200 | tf_op jit(solution)/shard_map/sqbc,sqbpj->spjc/dot_general | solution.py:53
  268.8 6.4 %copy.91 = bf16[2,2,4,32,4096]{4,0,1,3,2:T(2,128)(2,1)} copy(bf16[2,2,4,32,4096]{4,3,2,1,0:T(8,128)(2,1)S(1)} %bitcast.124) | data formatting | bytes 8388608 | tf_op jit(solution)/shard_map/reshape | solution.py:133
  275.2 30.8 %all-to-all-done.4 = bf16[2,2,4,32,4096]{4,0,1,3,2:T(2,128)(2,1)} async-done(((bf16[2,2,4,32,4096]{4,0,1,3,2:T(2,128)(2,1)}), bf16[2,2,4,32,4096]{4,0,1,3,2:T(2,128)(2,1)}, u32[]{:S(2)}, u32[]{:S(2)}) %all-to-all-start.4) | async-done | bytes 4194336 | tf_op jit(solution)/shard_map/all_to_all | solution.py:136
  311.1 6.5 %multiply_add_fusion.1 = (f32[2,1,128,4096]{3,2,1,0:T(8,128)S(1)}, f32[2,1,128,4096]{3,2,1,0:T(8,128)S(1)}) fusion(f32[2,2,128,4096]{3,2,1,0:T(8,128)} %convolution_bitcast_fusion, f32[2,2,128,4096]{3,2,1,0:T(8,128)} %convolution_bitcast_fusion.2), kind=kLoop, calls=%fused_computation.27 | loop fusion | flops 6291456 | bytes 25165824 | tf_op jit(solution)/shard_map/add | solution.py:67
  317.7 7.8 %fusion.2 = bf16[2,2,128,4096,1]{3,2,0,1,4:T(8,128)(2,1)S(1)} fusion(f32[2,1,128,4096]{3,2,1,0:T(8,128)S(1)} %get-tuple-element.12, f32[2,1,128,4096]{3,2,1,0:T(8,128)S(1)} %get-tuple-element.11, f32[2,1,128,2,128]{2,4,3,0,1:T(8,128)S(1)} %get-tuple-element.20, f32[2,1,128,2,128]{2,4,3,0,1:T(8,128)S(1)} %get-tuple-element.19), kind=kOutput, calls=%fused_computation.7 | convolution fusion | flops 6444679168 | bytes 13107200 | tf_op jit(solution)/shard_map/sqbc,sqbpj->spjc/dot_general | solution.py:53
  326.0 6.3 %copy.86 = bf16[2,2,4,32,4096]{4,0,1,3,2:T(2,128)(2,1)} copy(bf16[2,2,4,32,4096]{4,3,2,1,0:T(8,128)(2,1)S(1)} %bitcast.125) | data formatting | bytes 8388608 | tf_op jit(solution)/shard_map/reshape | solution.py:133
  332.3 25.7 %all-to-all-done.10 = bf16[2,2,4,32,4096]{4,0,1,3,2:T(2,128)(2,1)} async-done(((bf16[2,2,4,32,4096]{4,0,1,3,2:T(2,128)(2,1)}), bf16[2,2,4,32,4096]{4,0,1,3,2:T(2,128)(2,1)}, u32[]{:S(2)}, u32[]{:S(2)}) %all-to-all-start.10) | async-done | bytes 4194336 | tf_op jit(solution)/shard_map/all_to_all | solution.py:138
  363.3 10.8 %fusion.6 = bf16[4,32,4096]{2,0,1:T(4,128)(2,1)S(1)} fusion(bf16[2,2,4,32,4096]{4,0,1,3,2:T(2,128)(2,1)} %all-to-all-done.4, f32[4,2,1,4]{0,3,2,1:T(4,128)S(1)} %get-tuple-element.31, f32[4,2,1,4]{0,3,2,1:T(4,128)S(1)} %get-tuple-element.30), kind=kOutput, calls=%fused_computation.21 | convolution fusion | flops 101187712 | bytes 5243136 | tf_op jit(solution)/shard_map/lirgc,mlir->mgc/dot_general | solution.py:143
  375.7 34.5 %all-to-all-done.8 = bf16[2,2,4,32,4096]{4,0,1,3,2:T(2,128)(2,1)} async-done(((bf16[2,2,4,32,4096]{4,0,1,3,2:T(2,128)(2,1)}), bf16[2,2,4,32,4096]{4,0,1,3,2:T(2,128)(2,1)}, u32[]{:S(2)}, u32[]{:S(2)}) %all-to-all-start.8) | async-done | bytes 4194336 | tf_op jit(solution)/shard_map/all_to_all | solution.py:137
  413.8 10.8 %fusion.7 = bf16[4,32,4096]{2,0,1:T(4,128)(2,1)S(1)} fusion(bf16[2,2,4,32,4096]{4,0,1,3,2:T(2,128)(2,1)} %all-to-all-done.8, f32[4,2,1,4]{0,3,2,1:T(4,128)S(1)} %get-tuple-element.31, f32[4,2,1,4]{0,3,2,1:T(4,128)S(1)} %get-tuple-element.30), kind=kOutput, calls=%fused_computation.22 | convolution fusion | flops 101187712 | bytes 5243136 | tf_op jit(solution)/shard_map/lirgc,mlir->mgc/dot_general | solution.py:143
  430.4 22.3 %psum.7 = bf16[1,4096]{1,0:T(2,128)(2,1)S(1)} all-reduce(bf16[1,4096]{1,0:T(2,128)(2,1)S(1)} %broadcast_in_dim.5), channel_id=1, replica_groups=mesh['section'=8,'ctx'=4] {'ctx'}, use_global_device_ids=true, to_apply=%region_3.4 | all-reduce | flops 4096 | bytes 16384 | tf_op jit(solution)/shard_map/psum | solution.py:169
  453.3 10.8 %fusion.8 = bf16[4,32,4096]{2,0,1:T(4,128)(2,1)S(1)} fusion(bf16[2,2,4,32,4096]{4,0,1,3,2:T(2,128)(2,1)} %all-to-all-done.10, f32[4,2,1,4]{0,3,2,1:T(4,128)S(1)} %get-tuple-element.31, f32[4,2,1,4]{0,3,2,1:T(4,128)S(1)} %get-tuple-element.30), kind=kOutput, calls=%fused_computation.23 | convolution fusion | flops 101187712 | bytes 5243136 | tf_op jit(solution)/shard_map/lirgc,mlir->mgc/dot_general | solution.py:143
  479.8 8.2 %all-gather = bf16[16384]{0:T(1024)(128)(2,1)S(1)} all-gather(bf16[4096]{0:T(1024)(128)(2,1)S(1)} %negate_convert_fusion), channel_id=2, replica_groups=mesh['section'=8,'ctx'=4] {'ctx'}, dimensions={0}, use_global_device_ids=true | all-gather | bytes 40960 | tf_op jit(solution)/shard_map/all_gather | solution.py:168
  (73 shorter events, 129.4 us)
Async XLA Ops:
  0.6 8.7 %copy-start.3 = (bf16[1,128,4096]{2,1,0:T(8,128)(2,1)S(1)}, bf16[1,128,4096]{2,1,0:T(8,128)(2,1)}, u32[]{:S(2)}) copy-start(bf16[1,128,4096]{2,1,0:T(8,128)(2,1)} %param.13) | copy-start | bytes 3145732
  0.6 8.7 %copy-start.2 = (bf16[1,128,4096]{2,1,0:T(8,128)(2,1)S(1)}, bf16[1,128,4096]{2,1,0:T(8,128)(2,1)}, u32[]{:S(2)}) copy-start(bf16[1,128,4096]{2,1,0:T(8,128)(2,1)} %param.8) | copy-start | bytes 3145732
  4.2 18.8 %all-to-all-start = ((bf16[4,32,4096]{2,1,0:T(8,128)(2,1)}), bf16[4,32,4096]{2,1,0:T(8,128)(2,1)S(1)}, u32[]{:S(2)}, u32[]{:S(2)}) async-start(bf16[4,32,4096]{2,1,0:T(8,128)(2,1)} %fusion.21), calls=%async_computation | async-start | bytes 2097152 | tf_op jit(solution)/shard_map/all_to_all | solution.py:100
  23.0 16.6 %all-to-all-start.6 = ((bf16[4,32,4096]{2,1,0:T(8,128)(2,1)}), bf16[4,32,4096]{2,1,0:T(8,128)(2,1)S(1)}, u32[]{:S(2)}, u32[]{:S(2)}) async-start(bf16[4,32,4096]{2,1,0:T(8,128)(2,1)} %bitcast.32), calls=%async_computation.6 | async-start | bytes 2097152 | tf_op jit(solution)/shard_map/all_to_all | solution.py:103
  39.6 16.6 %all-to-all-start.2 = ((bf16[4,32,4096]{2,1,0:T(8,128)(2,1)}), bf16[4,32,4096]{2,1,0:T(8,128)(2,1)S(1)}, u32[]{:S(2)}, u32[]{:S(2)}) async-start(bf16[4,32,4096]{2,1,0:T(8,128)(2,1)} %bitcast.17), calls=%async_computation.2 | async-start | bytes 2097152 | tf_op jit(solution)/shard_map/all_to_all | solution.py:97
  56.2 51.9 %all-to-all-start.7 = ((bf16[2,2,4,32,4096]{4,3,1,0,2:T(8,128)(2,1)}), bf16[2,2,4,32,4096]{4,3,1,0,2:T(8,128)(2,1)}, u32[]{:S(2)}, u32[]{:S(2)}) async-start(bf16[2,2,4,32,4096]{4,3,1,0,2:T(8,128)(2,1)} %copy.83), calls=%async_computation.7 | async-start | bytes 8388608 | tf_op jit(solution)/shard_map/all_to_all | solution.py:119
  108.0 52.0 %all-to-all-start.1 = ((bf16[2,2,4,32,4096]{4,3,1,0,2:T(8,128)(2,1)}), bf16[2,2,4,32,4096]{4,3,1,0,2:T(8,128)(2,1)}, u32[]{:S(2)}, u32[]{:S(2)}) async-start(bf16[2,2,4,32,4096]{4,3,1,0,2:T(8,128)(2,1)} %copy.72), calls=%async_computation.1 | async-start | bytes 8388608 | tf_op jit(solution)/shard_map/all_to_all | solution.py:116
  160.0 52.2 %all-to-all-start.3 = ((bf16[2,2,4,32,4096]{4,3,1,0,2:T(8,128)(2,1)}), bf16[2,2,4,32,4096]{4,3,1,0,2:T(8,128)(2,1)}, u32[]{:S(2)}, u32[]{:S(2)}) async-start(bf16[2,2,4,32,4096]{4,3,1,0,2:T(8,128)(2,1)} %copy.75), calls=%async_computation.3 | async-start | bytes 8388608 | tf_op jit(solution)/shard_map/all_to_all | solution.py:113
  212.2 8.3 %slice-start = ((s8[8388608]{0:T(1024)(128)(4,1)}), s8[4194304]{0:T(1024)(128)(4,1)S(1)}, s32[]{:S(2)}) async-start(s8[8388608]{0:T(1024)(128)(4,1)} %bitcast.118), calls=%async_computation.12 | async-start | bytes 8388608
  214.8 5.7 %slice-start.1 = ((s8[8388608]{0:T(1024)(128)(4,1)}), s8[4194304]{0:T(1024)(128)(4,1)S(1)}, s32[]{:S(2)}) async-start(s8[8388608]{0:T(1024)(128)(4,1)} %bitcast.118), calls=%async_computation.13 | async-start | bytes 8388608
  254.0 52.0 %all-to-all-start.4 = ((bf16[2,2,4,32,4096]{4,0,1,3,2:T(2,128)(2,1)}), bf16[2,2,4,32,4096]{4,0,1,3,2:T(2,128)(2,1)}, u32[]{:S(2)}, u32[]{:S(2)}) async-start(bf16[2,2,4,32,4096]{4,0,1,3,2:T(2,128)(2,1)} %copy.78), calls=%async_computation.4 | async-start | bytes 8388608 | tf_op jit(solution)/shard_map/all_to_all | solution.py:136
  306.0 52.0 %all-to-all-start.10 = ((bf16[2,2,4,32,4096]{4,0,1,3,2:T(2,128)(2,1)}), bf16[2,2,4,32,4096]{4,0,1,3,2:T(2,128)(2,1)}, u32[]{:S(2)}, u32[]{:S(2)}) async-start(bf16[2,2,4,32,4096]{4,0,1,3,2:T(2,128)(2,1)} %copy.91), calls=%async_computation.10 | async-start | bytes 8388608 | tf_op jit(solution)/shard_map/all_to_all | solution.py:138
  358.0 52.2 %all-to-all-start.8 = ((bf16[2,2,4,32,4096]{4,0,1,3,2:T(2,128)(2,1)}), bf16[2,2,4,32,4096]{4,0,1,3,2:T(2,128)(2,1)}, u32[]{:S(2)}, u32[]{:S(2)}) async-start(bf16[2,2,4,32,4096]{4,0,1,3,2:T(2,128)(2,1)} %copy.86), calls=%async_computation.8 | async-start | bytes 8388608 | tf_op jit(solution)/shard_map/all_to_all | solution.py:137
  410.2 16.6 %all-to-all-start.5 = ((bf16[4,32,4096]{2,1,0:T(8,128)(2,1)}), bf16[4,32,4096]{2,1,0:T(8,128)(2,1)S(1)}, u32[]{:S(2)}, u32[]{:S(2)}) async-start(bf16[4,32,4096]{2,1,0:T(8,128)(2,1)} %copy.81), calls=%async_computation.5 | async-start | bytes 2097152 | tf_op jit(solution)/shard_map/all_to_all | solution.py:148
  426.9 38.9 %all-to-all-start.9 = ((bf16[4,32,4096]{2,1,0:T(8,128)(2,1)}), bf16[4,32,4096]{2,1,0:T(8,128)(2,1)S(1)}, u32[]{:S(2)}, u32[]{:S(2)}) async-start(bf16[4,32,4096]{2,1,0:T(8,128)(2,1)} %copy.89), calls=%async_computation.9 | async-start | bytes 2097152 | tf_op jit(solution)/shard_map/all_to_all | solution.py:149
  464.1 5.1 %copy-start.4 = (f32[1,4096]{1,0:T(1,128)S(1)}, f32[1,4096]{1,0:T(1,128)}, u32[]{:S(2)}) copy-start(f32[1,4096]{1,0:T(1,128)} %param.12) | copy-start | bytes 49156
  465.7 3.5 copy-start.1
  465.7 13.3 %all-to-all-start.11 = ((bf16[4,32,4096]{2,1,0:T(8,128)(2,1)}), bf16[4,32,4096]{2,1,0:T(8,128)(2,1)S(1)}, u32[]{:S(2)}, u32[]{:S(2)}) async-start(bf16[4,32,4096]{2,1,0:T(8,128)(2,1)} %copy.94), calls=%async_computation.11 | async-start | bytes 2097152 | tf_op jit(solution)/shard_map/all_to_all | solution.py:150
  469.3 9.7 %copy-start = (bf16[1,128,4096]{2,1,0:T(8,128)(2,1)S(1)}, bf16[1,128,4096]{2,1,0:T(8,128)(2,1)}, u32[]{:S(2)}) copy-start(bf16[1,128,4096]{2,1,0:T(8,128)(2,1)} %param.10) | copy-start | bytes 3145732
  474.8 15.4 %collective-permute-start = (bf16[1,128,4096]{2,1,0:T(8,128)(2,1)}, bf16[1,128,4096]{2,1,0:T(8,128)(2,1)S(1)}, u32[]{:S(2)}, u32[]{:S(2)}) collective-permute-start(bf16[1,128,4096]{2,1,0:T(8,128)(2,1)} %get-tuple-element.17), channel_id=1, source_target_pairs={{4,0},{8,4},{12,8},{16,12},{20,16},{24,20},{28,24},{5,1},{9,5},{13... | collective-permute-start | bytes 3145736 | tf_op jit(solution)/shard_map/ppermute | solution.py:13
